TPU v7x, 32 devices: a whole 2x2x4 slice. The times are simulated.
32 devices in a mesh: groups: 2 (over y), latent: 4 (over z), rows: 4 (over x, core).
Axes of the slice: x: 2, y: 2, z: 4, core: 2. Of those that a mesh axis runs over, the one named last changes fastest.
Arguments:
- activations_in: bfloat16 [2, 128, 2304], P('groups', None, 'latent'), parts along dimension 0, may hold values from -6 to 6
- gate_proj: bfloat16 [2304, 4608], P('rows', 'latent'), may hold values from -0.125 to 0.125
- up_proj: bfloat16 [2304, 4608], P('rows', 'latent'), may hold values from -0.125 to 0.125
- down_proj: bfloat16 [4608, 2304], P('latent', 'rows'), may hold values from -0.09375 to 0.09375
- enc_weight: bfloat16 [4608, 65536], P(('groups', 'rows'), 'latent'), parts along dimension 0, may hold values from -6 to 6
- enc_bias: float32 [131072], P(('groups', 'latent')), parts along dimension 0, may hold values from -0.5 to 0.5
- dec_weight: bfloat16 [131072, 2304], P(('groups', 'latent'), 'rows'), parts along dimension 0, may hold values from -6 to 6
- dec_bias: float32 [4608], P(('groups', 'rows')), parts along dimension 0, may hold values from -0.5 to 0.5
Outputs:
- enc_weight_new: bfloat16 [4608, 65536], P(('groups', 'rows'), 'latent'), parts along dimension 0
- enc_bias_new: float32 [131072], P(('groups', 'latent')), parts along dimension 0
- dec_weight_new: bfloat16 [131072, 2304], P(('groups', 'latent'), 'rows'), parts along dimension 0
- dec_bias_new: float32 [4608], P(('groups', 'rows')), parts along dimension 0
There are 2 independent parts, one for each index of `groups`. A program takes and returns all parts, laid end to end along the dimension named above; an argument that names none is the same for every part. Nothing has to cross between parts.
All inputs are finite; a program needn't handle non-finite values.
Results may differ from a plain program's by a relative error of at most 0.02.
Values may be sent and summed in bfloat16 or wider, within the bound.
A program may use at most 128 MiB of HBM per device.

v0:
```python
import jax
import jax.numpy as jnp
from jax import lax
from jax.sharding import PartitionSpec as P

MODEL_WIDTH = 2304
LATENTS = 65536
sparsity_cost = 0.1
sharpness = 8.0
weight_rate = 2.0
enc_bias_rate = 0.01
dec_bias_rate = 0.002


def row_total(term):
    return lax.psum(term.astype(jnp.bfloat16), "rows").astype(jnp.float32)


def body(activations_in, gate_proj, up_proj, down_proj, enc_weight, enc_bias, dec_weight, dec_bias):
    gate_full, up_full = (
        lax.all_gather(gate_proj, "rows", axis=0, tiled=True),
        lax.all_gather(up_proj, "rows", axis=0, tiled=True),
    )
    batches = activations_in.shape[0]
    batch_tokens = activations_in.shape[1]
    all_tokens = batches * batch_tokens
    token_rows = activations_in.reshape(all_tokens, activations_in.shape[2])
    portion = lax.all_gather(token_rows, "latent", axis=1, tiled=True)
    gate_term = jnp.dot(portion, gate_full, preferred_element_type=jnp.float32)
    up_term = jnp.dot(portion, up_full, preferred_element_type=jnp.float32)
    hidden = (jax.nn.gelu(gate_term, approximate=True) * up_term).astype(jnp.bfloat16)
    partial_value = jnp.dot(hidden, down_proj, preferred_element_type=jnp.float32)
    features = lax.psum(partial_value, "latent").astype(jnp.bfloat16)
    features = features.reshape(batches, batch_tokens, features.shape[1])
    enc_scale = MODEL_WIDTH ** (-0.5)
    dec_scale = LATENTS ** (-0.5)
    inputs = features[0]
    local_pre = jnp.dot(inputs, enc_weight, preferred_element_type=jnp.float32)
    pre_latent = enc_scale * row_total(local_pre) + enc_bias
    latents = (jax.nn.softplus(sharpness * pre_latent) / sharpness).astype(jnp.bfloat16)
    local_rebuilt = jnp.dot(latents, dec_weight, preferred_element_type=jnp.float32)
    rebuilt_share = lax.psum_scatter(local_rebuilt, "latent", scatter_dimension=1, tiled=True)
    share_cols = rebuilt_share.shape[1]
    col_offset = lax.axis_index("latent") * share_cols
    inputs_here = lax.dynamic_slice_in_dim(inputs, col_offset, share_cols, 1)
    bias_here = lax.dynamic_slice_in_dim(dec_bias, col_offset, share_cols, 0)
    grad_share = (
        2.0 * (dec_scale * rebuilt_share + bias_here - inputs_here.astype(jnp.float32))
    ).astype(jnp.bfloat16)
    residual_grad = lax.all_gather(grad_share, "latent", axis=1, tiled=True)
    local_back = lax.dot_general(
        residual_grad, dec_weight, (((1,), (1,)), ((), ())), preferred_element_type=jnp.float32
    )
    back_sum = row_total(local_back)
    latent_grad = (
        jax.nn.sigmoid(sharpness * pre_latent) * (dec_scale * back_sum + sparsity_cost)
    ).astype(jnp.bfloat16)
    dec_grad = dec_scale * lax.dot_general(
        latents, residual_grad, (((0,), (0,)), ((), ())), preferred_element_type=jnp.float32
    )
    enc_grad = enc_scale * lax.dot_general(
        inputs, latent_grad, (((0,), (0,)), ((), ())), preferred_element_type=jnp.float32
    )
    enc_bias = enc_bias - enc_bias_rate * jnp.sum(latent_grad, axis=0, dtype=jnp.float32)
    dec_bias = dec_bias - dec_bias_rate * jnp.sum(residual_grad, axis=0, dtype=jnp.float32)
    enc_weight = (enc_weight.astype(jnp.float32) - weight_rate * enc_grad).astype(jnp.bfloat16)
    dec_weight = (dec_weight.astype(jnp.float32) - weight_rate * dec_grad).astype(jnp.bfloat16)
    return (enc_weight, enc_bias, dec_weight, dec_bias)


def solution(mesh):
    return jax.shard_map(
        body,
        mesh=mesh,
        in_specs=(
            P("groups", None, "latent"),
            P("rows", "latent"),
            P("rows", "latent"),
            P("latent", "rows"),
            P(("groups", "rows"), "latent"),
            P(("groups", "latent")),
            P(("groups", "latent"), "rows"),
            P(("groups", "rows")),
        ),
        out_specs=(
            P(("groups", "rows"), "latent"),
            P(("groups", "latent")),
            P(("groups", "latent"), "rows"),
            P(("groups", "rows")),
        ),
        check_vma=False,
    )
```

profile of v0, /device:TPU:0, one launch (start us, length us, event | category | flops | bytes accessed | tf_op | source)
XLA Modules:
  0.0 395.9 jit_solution(4908214912626969955)
XLA Ops:
  7.2 0.0 copy-start
  7.2 0.0 all-gather.4.cloned.1.call-start
  7.2 0.7 all-gather.4.cloned.1.call-update
  7.9 0.0 all-gather.6.cloned.1.call-start
  8.0 0.7 all-gather.6.cloned.1.call-update
  8.7 0.0 all-reduce.4.cloned.1.call-start
  8.7 18.5 %all-gather = bf16[1,128,2304]{1,2,0:T(8,128)(2,1)S(1)} all-gather(bf16[1,128,576]{1,2,0:T(8,128)(2,1)} %param.8), channel_id=2, replica_groups=mesh['groups'=2,'latent'=4,'rows'=4] {'latent'}, dimensions={2}, use_global_device_ids=true | all-gather | bytes 737280 | tf_op jit(solution)/shard_map/all_gather | solution.py:28
  27.2 25.9 %all-gather.4.cloned.1.call-done = bf16[2304,1152]{1,0:T(8,128)(2,1)} async-done(((bf16[576,1152]{1,0:T(8,128)(2,1)}), bf16[2304,1152]{1,0:T(8,128)(2,1)}) %all-gather.4.cloned.1.call-update) | async-done | bytes 5308432 | tf_op jit(solution)/shard_map/all_gather | solution.py:21
  53.1 3.5 fusion.14
  56.6 38.9 %all-gather.6.cloned.1.call-done = bf16[2304,1152]{1,0:T(8,128)(2,1)} async-done(((bf16[576,1152]{1,0:T(8,128)(2,1)}), bf16[2304,1152]{1,0:T(8,128)(2,1)}) %all-gather.6.cloned.1.call-update) | async-done | bytes 5308432 | tf_op jit(solution)/shard_map/all_gather | solution.py:22
  95.5 0.0 copy-done
  95.5 4.0 fusion.3
  99.4 25.3 %all-reduce.7 = bf16[128,576]{0,1:T(8,128)(2,1)S(1)} all-reduce(f32[128,576]{0,1:T(8,128)S(1)} %fusion.3), channel_id=1, replica_groups=mesh['groups'=2,'latent'=4,'rows'=4] {'latent'}, use_global_device_ids=true, to_apply=%region_0.0 | all-reduce | flops 73728 | bytes 442368 | tf_op jit(solution)/shard_map/psum | solution.py:33
  124.7 0.0 copy-start.2
  124.8 12.0 %convolution_convert_fusion.1 = bf16[128,16384]{1,0:T(8,128)(2,1)} fusion(bf16[128,576]{0,1:T(8,128)(2,1)S(1)} %all-reduce.7, bf16[576,16384]{1,0:T(8,128)(2,1)} %param.12), kind=kOutput, calls=%fused_computation.4 | convolution fusion | flops 2418016256 | bytes 23216128 | tf_op jit(solution)/shard_map/dot_general | solution.py:38
  136.7 0.0 all-reduce.4.cloned.1.call-update
  136.8 0.0 copy-start.3
  136.8 0.2 reduce-scatter.2.cloned.1.call-start
  137.0 82.7 %all-reduce.4.cloned.1.call-done = bf16[128,16384]{1,0:T(8,128)(2,1)} async-done(((bf16[128,16384]{1,0:T(8,128)(2,1)}), bf16[128,16384]{1,0:T(8,128)(2,1)}) %all-reduce.4.cloned.1.call-update) | async-done | bytes 4194320 | tf_op jit(solution)/shard_map/psum | solution.py:16
  219.7 0.0 copy-done.2
  219.7 15.9 %fusion.25 = f32[128,576]{0,1:T(8,128)} fusion(bf16[16384,576]{0,1:T(8,128)(2,1)} %param.14, bf16[128,16384]{1,0:T(8,128)(2,1)} %all-reduce.4.cloned.1.call-done, f32[16384]{0:T(1024)S(1)} %copy-done.2), kind=kOutput, calls=%fused_computation.36 | convolution fusion | flops 2441084928 | bytes 23429120 | tf_op jit(solution)/shard_map/dot_general | solution.py:41
  235.6 0.0 reduce-scatter.2.cloned.1.call-update
  235.6 0.0 all-reduce.6.cloned.1.call-start
  235.7 0.0 copy-done.3
  235.7 0.1 dynamic_slice.6
  235.8 20.4 %reduce-scatter.2.cloned.1.call-done = f32[128,144]{0,1:T(8,128)} async-done(((f32[128,576]{0,1:T(8,128)}), f32[128,144]{0,1:T(8,128)}) %reduce-scatter.2.cloned.1.call-update) | async-done | bytes 73744 | tf_op jit(solution)/shard_map/reduce_scatter | solution.py:42
  256.2 1.0 multiply_convert_fusion.1
  257.1 13.5 %all_gather.15 = bf16[128,576]{0,1:T(8,128)(2,1)S(1)} all-gather(bf16[128,144]{0,1:T(8,128)(2,1)S(1)} %multiply_convert_fusion.1), channel_id=1, replica_groups=mesh['groups'=2,'latent'=4,'rows'=4] {'latent'}, dimensions={1}, use_global_device_ids=true | all-gather | bytes 184320 | tf_op jit(solution)/shard_map/all_gather | solution.py:50
  270.6 12.0 %convolution_convert_fusion = bf16[128,16384]{1,0:T(8,128)(2,1)} fusion(bf16[128,576]{0,1:T(8,128)(2,1)S(1)} %all_gather.15, bf16[16384,576]{0,1:T(8,128)(2,1)} %param.14), kind=kOutput, calls=%fused_computation.3 | convolution fusion | flops 2418016256 | bytes 23216128 | tf_op jit(solution)/shard_map/dot_general | solution.py:51
  282.6 0.1 convert_reduce_fusion.1
  282.7 0.0 all-reduce.6.cloned.1.call-update
  282.7 0.6 multiply_subtract_fusion.1
  283.3 32.5 %subtract_convert_fusion = bf16[16384,576]{0,1:T(8,128)(2,1)} fusion(bf16[16384,576]{0,1:T(8,128)(2,1)} %param.14, bf16[128,576]{0,1:T(8,128)(2,1)S(1)} %all_gather.15, bf16[128,16384]{1,0:T(8,128)(2,1)} %all-reduce.4.cloned.1.call-done, f32[16384]{0:T(1024)S(1)} %copy-done.2), kind=kOutput, calls=%fused_computation | convolution fusion | flops 2478833664 | bytes 42156032 | tf_op jit(solution)/shard_map/dot_general | solution.py:58
  315.8 50.7 %all-reduce.6.cloned.1.call-done = bf16[128,16384]{1,0:T(8,128)(2,1)} async-done(((bf16[128,16384]{1,0:T(8,128)(2,1)}), bf16[128,16384]{1,0:T(8,128)(2,1)}) %all-reduce.6.cloned.1.call-update) | async-done | bytes 4194320 | tf_op jit(solution)/shard_map/psum | solution.py:16
  366.5 7.7 %convert_reduce_fusion = (f32[16384]{0:T(1024)S(1)}, bf16[128,16384]{1,0:T(8,128)(2,1)}) fusion(bf16[128,16384]{1,0:T(8,128)(2,1)} %all-reduce.6.cloned.1.call-done, f32[16384]{0:T(1024)S(1)} %copy-done.2, bf16[128,16384]{1,0:T(8,128)(2,1)} %all-reduce.4.cloned.1.call-done), kind=kLoop, calls=%fused_computation.7 | loop fusion | flops 29343744 | bytes 12713984 | tf_op jit(solution)/shard_map/reduce_sum | solution.py:64
  374.2 0.0 copy-start.1
  374.2 14.5 %subtract_convert_fusion.1 = bf16[576,16384]{1,0:T(8,128)(2,1)} fusion(bf16[576,16384]{1,0:T(8,128)(2,1)} %param.12, bf16[128,576]{0,1:T(8,128)(2,1)S(1)} %all-reduce.7, bf16[128,16384]{1,0:T(8,128)(2,1)} %get-tuple-element.5), kind=kOutput, calls=%fused_computation.1 | convolution fusion | flops 2453667840 | bytes 42090496 | tf_op jit(solution)/shard_map/dot_general | solution.py:61
  388.7 0.6 multiply_subtract_fusion
  389.3 0.0 copy-done.1
Async XLA Ops:
  7.2 88.3 %copy-start = (bf16[1152,576]{0,1:T(8,128)(2,1)S(1)}, bf16[1152,576]{0,1:T(8,128)(2,1)}, u32[]{:S(2)}) copy-start(bf16[1152,576]{0,1:T(8,128)(2,1)} %param.11) | copy-start | bytes 3981316
  7.2 45.9 %all-gather.4.cloned.1.call-start = ((), (), s32[]{:S(2)}) async-start(), calls=%async_computation.1 | async-start | bytes 6635520 | tf_op jit(solution)/shard_map/all_gather | solution.py:21
  7.9 87.5 %all-gather.6.cloned.1.call-start = ((), (), s32[]{:S(2)}) async-start(), calls=%async_computation.2 | async-start | bytes 6635520 | tf_op jit(solution)/shard_map/all_gather | solution.py:22
  8.7 211.0 %all-reduce.4.cloned.1.call-start = ((), (), s32[]{:S(2)}) async-start(), calls=%async_computation.3 | async-start | bytes 8388608 | tf_op jit(solution)/shard_map/psum | solution.py:16
  124.7 94.9 %copy-start.2 = (f32[16384]{0:T(1024)S(1)}, f32[16384]{0:T(1024)}, u32[]{:S(2)}) copy-start(f32[16384]{0:T(1024)} %param.13) | copy-start | bytes 196612
  136.8 98.9 %copy-start.3 = (f32[576]{0:T(1024)S(1)}, f32[576]{0:T(1024)}, u32[]{:S(2)}) copy-start(f32[576]{0:T(1024)} %param.15) | copy-start | bytes 6916
  136.8 119.4 %reduce-scatter.2.cloned.1.call-start = ((), (), s32[]{:S(2)}) async-start(), calls=%async_computation.4 | async-start | bytes 368640 | tf_op jit(solution)/shard_map/reduce_scatter | solution.py:42
  235.6 130.9 %all-reduce.6.cloned.1.call-start = ((), (), s32[]{:S(2)}) async-start(), calls=%async_computation.5 | async-start | bytes 8388608 | tf_op jit(solution)/shard_map/psum | solution.py:16
  374.2 15.1 %copy-start.1 = (bf16[1152,576]{0,1:T(8,128)(2,1)S(1)}, bf16[1152,576]{0,1:T(8,128)(2,1)}, u32[]{:S(2)}) copy-start(bf16[1152,576]{0,1:T(8,128)(2,1)} %param.11) | copy-start | bytes 3981316
Sparse Core Ops, SparseCore 0:
  9.5 43.4 all-gather.3
  54.6 40.7 all-gather.5
  136.9 82.7 all-reduce.3
  235.8 20.3 reduce-scatter.1
  282.9 83.6 all-reduce.5
where the time goes:
time: 396 us
  waiting for transfers between devices  220 us (56%)
  matrix products  94.3 us (24%)
  blocking collectives  57.3 us (14%)
  between operations  13.8 us (3%)
  other arithmetic  10 us (3%)
    psum x2, waiting for transfers between devices, row_total(): return lax.psum(term.astype(jnp.bfloat16), 'rows').astype(jnp.float32)  133 us
    all_gather x1, waiting for transfers between devices, body(): lax.all_gather(up_proj, 'rows', axis=0, tiled=True)  38.9 us
    dot_general x1, matrix products, body(): lax.dot_general(latents, residual_grad, (((0,), (0,)), ((), ())), preferr...  32.5 us
    all_gather x1, waiting for transfers between devices, body(): lax.all_gather(gate_proj, 'rows', axis=0, tiled=True)  25.9 us
    psum x1, blocking collectives, body(): features = lax.psum(partial_value, 'latent').astype(jnp.bfloat16)  25.3 us
    reduce_scatter x1, waiting for transfers between devices, body(): lax.psum_scatter(local_rebuilt, 'latent', scatter_dimension=1, tiled=True)  20.4 us
    all_gather x1, blocking collectives, body(): portion = lax.all_gather(token_rows, 'latent', axis=1, tiled=True)  18.5 us
    dot_general x1, matrix products, body(): jnp.dot(latents, dec_weight, preferred_element_type=jnp.float32)  15.9 us
  transfers between devices with their start and end apart: 5, of which 5 were waited for; matrix products, arithmetic and copies ran while one was open for 9% of the time, Pallas kernels for 0%

commit v1 on v0

--- a/solution.py
+++ b/solution.py
@@ -30,7 +30,7 @@
     up_term = jnp.dot(portion, up_full, preferred_element_type=jnp.float32)
     hidden = (jax.nn.gelu(gate_term, approximate=True) * up_term).astype(jnp.bfloat16)
     partial_value = jnp.dot(hidden, down_proj, preferred_element_type=jnp.float32)
-    features = lax.psum(partial_value, "latent").astype(jnp.bfloat16)
+    features = jnp.sum(lax.all_gather(partial_value, "latent"), axis=0).astype(jnp.bfloat16)
     features = features.reshape(batches, batch_tokens, features.shape[1])
     enc_scale = MODEL_WIDTH ** (-0.5)
     dec_scale = LATENTS ** (-0.5)

time: 396 us -> 407 us (1.028)
  waiting for transfers between devices: 220 us -> 253 us
  blocking collectives: 57.3 us -> 32 us
    all_gather x0 -> x1, waiting for transfers between devices: none -> 31.8 us  [body(): lax.all_gather(partial_value, 'latent')]
    psum x1 -> x0, blocking collectives: 25.3 us -> none  [body(): features = lax.psum(partial_value, 'latent').astype(jnp.bfloat16)]
  transfers between devices with their start and end apart: 5 -> 6, of which waited for: 5 -> 6; matrix products, arithmetic and copies ran while one was open for 9% -> 9% of each run, Pallas kernels for 0% -> 0%
where the time goes in v1:
time: 407 us
  waiting for transfers between devices  253 us (62%)
  matrix products  95 us (23%)
  blocking collectives  32 us (8%)
  between operations  14.2 us (3%)
  other arithmetic  10.7 us (3%)
    psum x2, waiting for transfers between devices, row_total(): return lax.psum(term.astype(jnp.bfloat16), 'rows').astype(jnp.float32)  134 us
    all_gather x1, waiting for transfers between devices, body(): lax.all_gather(up_proj, 'rows', axis=0, tiled=True)  38.9 us
    dot_general x1, matrix products, body(): lax.dot_general(latents, residual_grad, (((0,), (0,)), ((), ())), preferr...  32.5 us
    all_gather x1, waiting for transfers between devices, body(): lax.all_gather(partial_value, 'latent')  31.8 us
    all_gather x1, waiting for transfers between devices, body(): lax.all_gather(gate_proj, 'rows', axis=0, tiled=True)  25.9 us
    reduce_scatter x1, waiting for transfers between devices, body(): lax.psum_scatter(local_rebuilt, 'latent', scatter_dimension=1, tiled=True)  20.4 us
    all_gather x1, blocking collectives, body(): portion = lax.all_gather(token_rows, 'latent', axis=1, tiled=True)  18.5 us
    dot_general x1, matrix products, body(): jnp.dot(latents, dec_weight, preferred_element_type=jnp.float32)  15.9 us
  transfers between devices with their start and end apart: 6, of which 6 were waited for; matrix products, arithmetic and copies ran while one was open for 9% of the time, Pallas kernels for 0%

profile of v1, /device:TPU:0, one launch (start us, length us, event | category | flops | bytes accessed | tf_op | source)
XLA Modules:
  0.0 406.9 jit_solution(7723960838168735028)
XLA Ops:
  7.2 0.0 copy-start
  7.2 0.0 all-gather.6.cloned.1.call-start
  7.2 0.7 all-gather.6.cloned.1.call-update
  7.9 0.0 all-gather.8.cloned.1.call-start
  8.0 0.7 all-gather.8.cloned.1.call-update
  8.7 0.0 all-gather.10.cloned.1.call-start
  8.7 18.5 %all-gather = bf16[1,128,2304]{1,2,0:T(8,128)(2,1)S(1)} all-gather(bf16[1,128,576]{1,2,0:T(8,128)(2,1)} %param.8), channel_id=2, replica_groups=mesh['groups'=2,'latent'=4,'rows'=4] {'latent'}, dimensions={2}, use_global_device_ids=true | all-gather | bytes 737280 | tf_op jit(solution)/shard_map/all_gather | solution.py:28
  27.2 25.9 %all-gather.6.cloned.1.call-done = bf16[2304,1152]{1,0:T(8,128)(2,1)} async-done(((bf16[576,1152]{1,0:T(8,128)(2,1)}), bf16[2304,1152]{1,0:T(8,128)(2,1)}) %all-gather.6.cloned.1.call-update) | async-done | bytes 5308432 | tf_op jit(solution)/shard_map/all_gather | solution.py:21
  53.1 3.5 fusion.14
  56.6 38.9 %all-gather.8.cloned.1.call-done = bf16[2304,1152]{1,0:T(8,128)(2,1)} async-done(((bf16[576,1152]{1,0:T(8,128)(2,1)}), bf16[2304,1152]{1,0:T(8,128)(2,1)}) %all-gather.8.cloned.1.call-update) | async-done | bytes 5308432 | tf_op jit(solution)/shard_map/all_gather | solution.py:22
  95.5 0.0 copy-done
  95.5 4.7 %fusion.3 = f32[128,576]{0,1:T(8,128)} fusion(bf16[1152,576]{0,1:T(8,128)(2,1)S(1)} %copy-done, bf16[2304,1152]{1,0:T(8,128)(2,1)} %all-gather.8.cloned.1.call-done, f32[128,1152]{1,0:T(8,128)S(1)} %fusion.14, bf16[1,128,2304]{1,2,0:T(8,128)(2,1)S(1)} %all-gather), kind=kOutput, calls=%fused_computation.12 | convolution fusion | flops 850821120 | bytes 8110080 | tf_op jit(solution)/shard_map/dot_general | solution.py:32
  100.1 0.0 all-gather.10.cloned.1.call-update
  100.2 0.0 all-reduce.3.cloned.1.call-start
  100.2 31.8 %all-gather.10.cloned.1.call-done = f32[512,576]{0,1:T(8,128)} async-done(((f32[128,576]{0,1:T(8,128)}), f32[512,576]{0,1:T(8,128)}) %all-gather.10.cloned.1.call-update) | async-done | bytes 1179664 | tf_op jit(solution)/shard_map/all_gather | solution.py:33
  132.0 1.7 reshape.15
  133.7 0.8 reduce_sum.27
  134.5 0.0 copy-start.2
  134.5 12.0 %convolution_convert_fusion.1 = bf16[128,16384]{1,0:T(8,128)(2,1)} fusion(bf16[128,576]{0,1:T(8,128)(2,1)S(1)} %reduce_sum.27, bf16[576,16384]{1,0:T(8,128)(2,1)} %param.12), kind=kOutput, calls=%fused_computation.4 | convolution fusion | flops 2418016256 | bytes 23216128 | tf_op jit(solution)/shard_map/dot_general | solution.py:38
  146.4 0.0 all-reduce.3.cloned.1.call-update
  146.5 0.0 copy-start.3
  146.5 0.2 reduce-scatter.2.cloned.1.call-start
  146.7 83.7 %all-reduce.3.cloned.1.call-done = bf16[128,16384]{1,0:T(8,128)(2,1)} async-done(((bf16[128,16384]{1,0:T(8,128)(2,1)}), bf16[128,16384]{1,0:T(8,128)(2,1)}) %all-reduce.3.cloned.1.call-update) | async-done | bytes 4194320 | tf_op jit(solution)/shard_map/psum | solution.py:16
  230.5 0.0 copy-done.2
  230.5 15.9 %fusion.25 = f32[128,576]{0,1:T(8,128)} fusion(bf16[16384,576]{0,1:T(8,128)(2,1)} %param.14, bf16[128,16384]{1,0:T(8,128)(2,1)} %all-reduce.3.cloned.1.call-done, f32[16384]{0:T(1024)S(1)} %copy-done.2), kind=kOutput, calls=%fused_computation.36 | convolution fusion | flops 2441084928 | bytes 23429120 | tf_op jit(solution)/shard_map/dot_general | solution.py:41
  246.4 0.0 reduce-scatter.2.cloned.1.call-update
  246.4 0.0 all-reduce.5.cloned.1.call-start
  246.5 0.0 copy-done.3
  246.5 0.1 dynamic_slice.6
  246.5 20.4 %reduce-scatter.2.cloned.1.call-done = f32[128,144]{0,1:T(8,128)} async-done(((f32[128,576]{0,1:T(8,128)}), f32[128,144]{0,1:T(8,128)}) %reduce-scatter.2.cloned.1.call-update) | async-done | bytes 73744 | tf_op jit(solution)/shard_map/reduce_scatter | solution.py:42
  266.9 1.0 multiply_convert_fusion.1
  267.9 13.5 %all_gather.23 = bf16[128,576]{0,1:T(8,128)(2,1)S(1)} all-gather(bf16[128,144]{0,1:T(8,128)(2,1)S(1)} %multiply_convert_fusion.1), channel_id=1, replica_groups=mesh['groups'=2,'latent'=4,'rows'=4] {'latent'}, dimensions={1}, use_global_device_ids=true | all-gather | bytes 184320 | tf_op jit(solution)/shard_map/all_gather | solution.py:50
  281.4 12.0 %convolution_convert_fusion = bf16[128,16384]{1,0:T(8,128)(2,1)} fusion(bf16[128,576]{0,1:T(8,128)(2,1)S(1)} %all_gather.23, bf16[16384,576]{0,1:T(8,128)(2,1)} %param.14), kind=kOutput, calls=%fused_computation.3 | convolution fusion | flops 2418016256 | bytes 23216128 | tf_op jit(solution)/shard_map/dot_general | solution.py:51
  293.3 0.1 convert_reduce_fusion.1
  293.5 0.0 all-reduce.5.cloned.1.call-update
  293.5 0.6 multiply_subtract_fusion.1
  294.1 32.5 %subtract_convert_fusion = bf16[16384,576]{0,1:T(8,128)(2,1)} fusion(bf16[16384,576]{0,1:T(8,128)(2,1)} %param.14, bf16[128,576]{0,1:T(8,128)(2,1)S(1)} %all_gather.23, bf16[128,16384]{1,0:T(8,128)(2,1)} %all-reduce.3.cloned.1.call-done, f32[16384]{0:T(1024)S(1)} %copy-done.2), kind=kOutput, calls=%fused_computation | convolution fusion | flops 2478833664 | bytes 42156032 | tf_op jit(solution)/shard_map/dot_general | solution.py:58
  326.6 50.7 %all-reduce.5.cloned.1.call-done = bf16[128,16384]{1,0:T(8,128)(2,1)} async-done(((bf16[128,16384]{1,0:T(8,128)(2,1)}), bf16[128,16384]{1,0:T(8,128)(2,1)}) %all-reduce.5.cloned.1.call-update) | async-done | bytes 4194320 | tf_op jit(solution)/shard_map/psum | solution.py:16
  377.3 7.6 %convert_reduce_fusion = (f32[16384]{0:T(1024)S(1)}, bf16[128,16384]{1,0:T(8,128)(2,1)}) fusion(bf16[128,16384]{1,0:T(8,128)(2,1)} %all-reduce.5.cloned.1.call-done, f32[16384]{0:T(1024)S(1)} %copy-done.2, bf16[128,16384]{1,0:T(8,128)(2,1)} %all-reduce.3.cloned.1.call-done), kind=kLoop, calls=%fused_computation.7 | loop fusion | flops 29343744 | bytes 12713984 | tf_op jit(solution)/shard_map/reduce_sum | solution.py:64
  384.9 0.0 copy-start.1
  384.9 14.5 %subtract_convert_fusion.1 = bf16[576,16384]{1,0:T(8,128)(2,1)} fusion(bf16[576,16384]{1,0:T(8,128)(2,1)} %param.12, bf16[128,576]{0,1:T(8,128)(2,1)S(1)} %reduce_sum.27, bf16[128,16384]{1,0:T(8,128)(2,1)} %get-tuple-element.5), kind=kOutput, calls=%fused_computation.1 | convolution fusion | flops 2453667840 | bytes 42090496 | tf_op jit(solution)/shard_map/dot_general | solution.py:61
  399.4 0.6 multiply_subtract_fusion
  400.0 0.0 copy-done.1
Async XLA Ops:
  7.2 88.3 %copy-start = (bf16[1152,576]{0,1:T(8,128)(2,1)S(1)}, bf16[1152,576]{0,1:T(8,128)(2,1)}, u32[]{:S(2)}) copy-start(bf16[1152,576]{0,1:T(8,128)(2,1)} %param.11) | copy-start | bytes 3981316
  7.2 45.9 %all-gather.6.cloned.1.call-start = ((), (), s32[]{:S(2)}) async-start(), calls=%async_computation.1 | async-start | bytes 6635520 | tf_op jit(solution)/shard_map/all_gather | solution.py:21
  7.9 87.5 %all-gather.8.cloned.1.call-start = ((), (), s32[]{:S(2)}) async-start(), calls=%async_computation.2 | async-start | bytes 6635520 | tf_op jit(solution)/shard_map/all_gather | solution.py:22
  8.7 123.4 %all-gather.10.cloned.1.call-start = ((), (), s32[]{:S(2)}) async-start(), calls=%async_computation.6 | async-start | bytes 1474560 | tf_op jit(solution)/shard_map/all_gather | solution.py:33
  100.2 130.3 %all-reduce.3.cloned.1.call-start = ((), (), s32[]{:S(2)}) async-start(), calls=%async_computation.3 | async-start | bytes 8388608 | tf_op jit(solution)/shard_map/psum | solution.py:16
  134.5 96.0 %copy-start.2 = (f32[16384]{0:T(1024)S(1)}, f32[16384]{0:T(1024)}, u32[]{:S(2)}) copy-start(f32[16384]{0:T(1024)} %param.13) | copy-start | bytes 196612
  146.5 100.0 %copy-start.3 = (f32[576]{0:T(1024)S(1)}, f32[576]{0:T(1024)}, u32[]{:S(2)}) copy-start(f32[576]{0:T(1024)} %param.15) | copy-start | bytes 6916
  146.5 120.4 %reduce-scatter.2.cloned.1.call-start = ((), (), s32[]{:S(2)}) async-start(), calls=%async_computation.4 | async-start | bytes 368640 | tf_op jit(solution)/shard_map/reduce_scatter | solution.py:42
  246.4 130.9 %all-reduce.5.cloned.1.call-start = ((), (), s32[]{:S(2)}) async-start(), calls=%async_computation.5 | async-start | bytes 8388608 | tf_op jit(solution)/shard_map/psum | solution.py:16
  384.9 15.1 %copy-start.1 = (bf16[1152,576]{0,1:T(8,128)(2,1)S(1)}, bf16[1152,576]{0,1:T(8,128)(2,1)}, u32[]{:S(2)}) copy-start(bf16[1152,576]{0,1:T(8,128)(2,1)} %param.11) | copy-start | bytes 3981316
Sparse Core Ops, SparseCore 0:
  9.5 43.4 all-gather.5
  54.6 40.7 all-gather.7
  100.3 31.7 all-gather.9
  146.6 83.8 all-reduce.2
  246.5 20.3 reduce-scatter.1
  293.6 83.6 all-reduce.4
